TPU v7x, 512 devices: a whole 4x4x16 slice. The times are simulated.
512 devices in a mesh: section: 8 (over x, core), seq: 16 (over z), chan: 4 (over y).
Axes of the slice: x: 4, y: 4, z: 16, core: 2. Of those that a mesh axis runs over, the one named last changes fastest.
Arguments:
- saved_input: bfloat16 [8, 2, 2048, 1024], P('section', None, 'seq', 'chan'), may hold values from -6 to 6
- pre_gate: bfloat16 [8, 2, 2048, 1024], P('section', None, 'seq', 'chan'), may hold values from -6 to 6
- post_gate: bfloat16 [8, 2, 2048, 1024], P('section', None, 'seq', 'chan'), may hold values from -6 to 6
- grad_held: bfloat16 [8, 2048, 1024], P('section', 'seq', 'chan'), may hold values from -6 to 6
- loss_grad: bfloat16 [2048, 1024], P('seq', 'chan'), may hold values from -6 to 6
- filters: float32 [8, 2048, 256], P('section', 'seq'), may hold values from -1 to 1
- skip_gain: float32 [8, 256], P('section'), may hold values from 0.5 to 1.5
Outputs:
- grad_out: bfloat16 [8, 2048, 1024], P('section', 'seq', 'chan')
- filter_grad: float32 [8, 2048, 256], P('section', 'seq', 'chan')
All inputs are finite; a program needn't handle non-finite values.
Results may differ from a plain program's by a relative error of at most 0.017.
Values may be sent and summed in bfloat16 or wider, within the bound.
A program may use at most 64 MiB of HBM per device.

v0:
```python
import functools
import math

import jax
import jax.numpy as jnp
from jax import lax
from jax.experimental import pallas as pl
from jax.experimental.pallas import tpu as pltpu
from jax.sharding import PartitionSpec as P

LANES = 128


def kernel(
    sections,
    n,
    chans,
    scale,
    saved,
    pre,
    post,
    grad_held,
    loss_grad,
    filters,
    gain,
    grad_out,
    filter_out,
    send_a,
    recv_a,
    send_b,
    recv_b,
    send_c,
    recv_c,
    send_d,
    recv_d,
    send_e,
    recv_e,
    send_f,
    recv_f,
    send_g,
    recv_g,
    carried,
    rows,
    padded,
    left,
    hankel,
    result,
    partial,
    send_sem,
    recv_sem,
    shift_sem,
):
    section = lax.axis_index("section")
    me = lax.axis_index("seq")
    chan = lax.axis_index("chan")
    width = grad_held.shape[1]
    own = width // n
    per_chan = n // chans
    owner_chan = me // per_chan
    keeps_own = owner_chan == chan
    order = sorted(range(1, n), key=lambda off: -min(off, n - off))

    barrier = pltpu.get_barrier_semaphore()
    for off in order:
        pl.semaphore_signal(barrier, inc=1, device_id={"seq": lax.rem(me + off, n)})

    @pl.when(section < sections - 1)
    def _():
        pl.semaphore_signal(barrier, inc=1, device_id={"section": section + 1})

    for slot in range(n):
        source = chan * per_chan + slot // chans

        @pl.when(jnp.logical_not((source == me) & (slot % chans == chan)))
        def _():
            pl.semaphore_signal(
                barrier, inc=1, device_id={"seq": source, "chan": jnp.int32(slot % chans)}
            )

    row_index = lax.broadcasted_iota(jnp.int32, (LANES, LANES), 0)
    lane_index = lax.broadcasted_iota(jnp.int32, (LANES, LANES), 1)
    flip = (row_index + lane_index == LANES - 1).astype(jnp.bfloat16)
    keep = lane_index <= row_index

    def by_channel(values):
        return jnp.transpose(values).astype(jnp.bfloat16)

    def flipped(values):
        turned = jnp.dot(by_channel(values), flip, preferred_element_type=jnp.float32)
        return turned.astype(jnp.bfloat16)

    gated_0 = post[0].astype(jnp.float32) * grad_held[...].astype(jnp.float32)
    send_a[:, 0] = by_channel(gated_0).reshape(n, own, LANES)
    send_a[:, 1] = flipped(filters[...]).reshape(n, own, LANES)
    for tick in range(2):
        mixed = pre[tick].astype(jnp.float32) * saved[tick].astype(jnp.float32)
        send_b[:, tick] = flipped(mixed).reshape(n, own, LANES)

    def exchange(src, dst, phase):
        copies = []
        for off in order:
            peer = lax.rem(me + off, n)
            copy = pltpu.make_async_remote_copy(
                src_ref=src.at[peer],
                dst_ref=dst.at[me],
                send_sem=send_sem.at[phase, off],
                recv_sem=recv_sem.at[phase, off],
                device_id={"seq": peer},
            )
            copy.start()
            copies.append(copy)
        dst[me] = src[me]
        return copies

    waiting = (
        n - 1 + n + (section > 0).astype(jnp.int32) - keeps_own.astype(jnp.int32)
    )
    pl.semaphore_wait(barrier, waiting)

    sent = []

    def arrive(copies):
        for copy in copies:
            copy.wait_recv()
        sent.extend(copies)

    def build_left(block, which):
        for m in range(n):
            padded[:, n - 1 - m, :] = block(m).astype(jnp.float32)

        def one(ch, carry):
            for m in range(n):
                left[which, ch, :, m * LANES : (m + 1) * LANES] = padded[
                    ch, n - 1 - m : 2 * n - 1 - m, :
                ].astype(jnp.bfloat16)
            return carry

        lax.fori_loop(0, own, one, 0)

    def correlate(block, send):
        for m in range(n):
            rows[:, m, :] = block(m).astype(jnp.float32)

        def one(ch, carry):
            held = rows[ch]

            def turned(m):
                spread = jnp.broadcast_to(held[m : m + 1], (LANES, LANES))
                return pltpu.roll(spread, 1, 1, stride=1, stride_axis=0)

            now = turned(0)
            for m in range(n):
                later = turned(m + 1) if m + 1 < n else jnp.zeros_like(now)
                hankel[ch, m * LANES : (m + 1) * LANES, :] = jnp.where(
                    keep, now, later
                ).astype(jnp.bfloat16)
                now = later
            result[ch] = jnp.dot(left[0, ch], hankel[ch], preferred_element_type=jnp.float32)
            return carry

        lax.fori_loop(0, own, one, 0)
        for m in range(n):
            send[m] = result[:, m, :].astype(jnp.bfloat16)

    def lag_products(tick):
        def one(ch, carry):
            product = jnp.dot(
                left[1 + tick, ch], hankel[ch], preferred_element_type=jnp.float32
            )
            if tick == 0:
                partial[ch] = product
            else:
                partial[ch] = partial[ch] + product
            return carry

        lax.fori_loop(0, own, one, 0)

    def combined(tick, held, gated, recv):
        back = jnp.transpose(recv[...].astype(jnp.float32).reshape(width, LANES))
        inner = back + gain[...] * gated
        return (held + pre[tick].astype(jnp.float32) * inner).astype(jnp.bfloat16)

    copies_a = exchange(send_a, recv_a, 0)
    copies_b = exchange(send_b, recv_b, 1)
    padded[:, n:, :] = jnp.zeros((own, n, LANES), jnp.float32)
    arrive(copies_a)
    build_left(lambda m: recv_a[m, 1], 0)
    correlate(lambda m: recv_a[m, 0], send_c)
    copies_c = exchange(send_c, recv_c, 2)
    arrive(copies_b)
    build_left(lambda m: recv_b[m, 0], 1)
    lag_products(0)
    arrive(copies_c)
    send_g[...] = combined(0, grad_held[...].astype(jnp.float32), gated_0, recv_c)
    shift = pltpu.make_async_remote_copy(
        src_ref=send_g,
        dst_ref=recv_g,
        send_sem=shift_sem.at[0],
        recv_sem=shift_sem.at[1],
        device_id={"section": lax.rem(section + sections - 1, sections)},
    )

    @pl.when(section > 0)
    def _():
        shift.start()

    build_left(lambda m: recv_b[m, 1], 2)

    @pl.when(section < sections - 1)
    def _():
        shift.wait_recv()
        carried[...] = recv_g[...].astype(jnp.float32)

    @pl.when(section == sections - 1)
    def _():
        carried[...] = loss_grad[...].astype(jnp.float32)

    gated_1 = post[1].astype(jnp.float32) * carried[...]
    send_d[...] = by_channel(gated_1).reshape(n, own, LANES)
    copies_d = exchange(send_d, recv_d, 3)
    arrive(copies_d)
    correlate(lambda m: recv_d[m], send_e)
    copies_e = exchange(send_e, recv_e, 4)
    lag_products(1)
    for m in range(n):
        send_f[m] = partial[:, m, :].astype(jnp.bfloat16)

    landing = lax.rem(me, per_chan) * chans + chan

    def deliver(off):
        target = lax.rem(me + off, n)
        return pltpu.make_async_remote_copy(
            src_ref=send_f.at[target],
            dst_ref=recv_f.at[landing],
            send_sem=send_sem.at[5, off],
            recv_sem=recv_sem.at[5, landing],
            device_id={"seq": target, "chan": owner_chan},
        )

    for off in order:
        deliver(off).start()

    @pl.when(jnp.logical_not(keeps_own))
    def _():
        deliver(0).start()

    @pl.when(keeps_own)
    def _():
        recv_f[landing] = send_f[me]

    arrive(copies_e)
    grad_out[...] = combined(1, carried[...], gated_1, recv_e)

    for slot in range(n):
        source = chan * per_chan + slot // chans

        @pl.when(jnp.logical_not((source == me) & (slot % chans == chan)))
        def _():
            pltpu.make_async_remote_copy(
                src_ref=send_f.at[0],
                dst_ref=recv_f.at[slot],
                send_sem=send_sem.at[5, 0],
                recv_sem=recv_sem.at[5, slot],
                device_id={"seq": source, "chan": jnp.int32(slot % chans)},
            ).wait_recv()

    pieces = recv_f[...].astype(jnp.float32).reshape(per_chan, chans, own, LANES)
    total = jnp.sum(pieces, axis=1).reshape(per_chan * own, LANES)
    filter_out[...] = jnp.transpose(total) * scale

    for copy in sent:
        copy.wait_send()

    @pl.when(section > 0)
    def _():
        shift.wait_send()

    for off in order:
        deliver(off).wait_send()

    @pl.when(jnp.logical_not(keeps_own))
    def _():
        deliver(0).wait_send()


def body(mesh, saved_input, pre_gate, post_gate, grad_held, loss_grad, filters, skip_gain):
    sections, n, chans = (mesh.shape[axis] for axis in ("section", "seq", "chan"))
    ticks, rows, width = saved_input.shape[1:]
    own = width // n
    length = rows * n
    scale = 1.0 / math.sqrt(length * chans * ticks)
    pair = pltpu.VMEM((n, 2, own, rows), jnp.bfloat16)
    single = pltpu.VMEM((n, own, rows), jnp.bfloat16)
    vmem = pl.BlockSpec(memory_space=pltpu.VMEM)
    gradient, lag_grad = pl.pallas_call(
        functools.partial(kernel, sections, n, chans, scale),
        out_shape=(
            jax.ShapeDtypeStruct((rows, width), jnp.bfloat16),
            jax.ShapeDtypeStruct((rows, width // chans), jnp.float32),
        ),
        in_specs=[vmem] * 7,
        out_specs=(vmem, vmem),
        scratch_shapes=[
            pair,
            pair,
            pair,
            pair,
            single,
            single,
            single,
            single,
            single,
            single,
            single,
            single,
            pltpu.VMEM((rows, width), jnp.bfloat16),
            pltpu.VMEM((rows, width), jnp.bfloat16),
            pltpu.VMEM((rows, width), jnp.float32),
            pltpu.VMEM((own, n, rows), jnp.float32),
            pltpu.VMEM((own, 2 * n, rows), jnp.float32),
            pltpu.VMEM((3, own, n, length), jnp.bfloat16),
            pltpu.VMEM((own, length, rows), jnp.bfloat16),
            pltpu.VMEM((own, n, rows), jnp.float32),
            pltpu.VMEM((own, n, rows), jnp.float32),
            pltpu.SemaphoreType.DMA((6, n)),
            pltpu.SemaphoreType.DMA((6, n)),
            pltpu.SemaphoreType.DMA((2,)),
        ],
        compiler_params=pltpu.CompilerParams(
            collective_id=0, has_side_effects=True, vmem_limit_bytes=48 * 1024 * 1024
        ),
    )(
        saved_input[0],
        pre_gate[0],
        post_gate[0],
        grad_held[0],
        loss_grad,
        filters[0],
        skip_gain,
    )
    return gradient[None], lag_grad[None]


def solution(mesh):
    placed = (
        P("section", None, "seq", "chan"),
        P("section", None, "seq", "chan"),
        P("section", None, "seq", "chan"),
        P("section", "seq", "chan"),
        P("seq", "chan"),
        P("section", "seq", None),
        P("section", None),
    )
    return jax.shard_map(
        functools.partial(body, mesh),
        mesh=mesh,
        in_specs=placed,
        out_specs=(P("section", "seq", "chan"), P("section", "seq", "chan")),
        check_vma=False,
    )
```

profile of v0, /device:TPU:19, one launch (start us, length us, event | category | flops | bytes accessed | tf_op | source)
XLA Modules:
  0.0 75.5 jit_solution(16917165446780523737)
XLA Ops:
  0.6 0.0 copy-start.6
  0.6 0.7 copy-done.6
  1.3 0.0 copy-start
  1.3 0.9 %copy-done = bf16[1,2,128,256]{3,2,1,0:T(8,128)(2,1)S(1)} copy-done((bf16[1,2,128,256]{3,2,1,0:T(8,128)(2,1)S(1)}, bf16[1,2,128,256]{3,2,1,0:T(8,128)(2,1)}, u32[]{:S(2)}) %copy-start) | copy-done | bytes 131096
  2.2 0.0 copy-start.1
  2.2 0.9 %copy-done.1 = bf16[1,2,128,256]{3,2,1,0:T(8,128)(2,1)S(1)} copy-done((bf16[1,2,128,256]{3,2,1,0:T(8,128)(2,1)S(1)}, bf16[1,2,128,256]{3,2,1,0:T(8,128)(2,1)}, u32[]{:S(2)}) %copy-start.1) | copy-done | bytes 131096
  3.1 0.0 copy-start.2
  3.1 0.9 %copy-done.2 = bf16[1,2,128,256]{3,2,1,0:T(8,128)(2,1)S(1)} copy-done((bf16[1,2,128,256]{3,2,1,0:T(8,128)(2,1)S(1)}, bf16[1,2,128,256]{3,2,1,0:T(8,128)(2,1)}, u32[]{:S(2)}) %copy-start.2) | copy-done | bytes 131096
  4.0 0.0 copy-start.3
  4.0 0.9 %copy-done.3 = f32[1,128,256]{2,1,0:T(8,128)S(1)} copy-done((f32[1,128,256]{2,1,0:T(8,128)S(1)}, f32[1,128,256]{2,1,0:T(8,128)}, u32[]{:S(2)}) %copy-start.3) | copy-done | bytes 131096
  4.9 0.0 copy-start.4
  4.9 0.8 %copy-done.4 = bf16[1,128,256]{2,1,0:T(8,128)(2,1)S(1)} copy-done((bf16[1,128,256]{2,1,0:T(8,128)(2,1)S(1)}, bf16[1,128,256]{2,1,0:T(8,128)(2,1)}, u32[]{:S(2)}) %copy-start.4) | copy-done | bytes 65560
  5.8 0.0 copy-start.5
  5.8 0.8 %copy-done.5 = bf16[128,256]{1,0:T(8,128)(2,1)S(1)} copy-done((bf16[128,256]{1,0:T(8,128)(2,1)S(1)}, bf16[128,256]{1,0:T(8,128)(2,1)}, u32[]{:S(2)}) %copy-start.5) | copy-done | bytes 65560
  6.6 67.5 %shard_map.86 = (bf16[128,256]{1,0:T(8,128)(2,1)S(1)}, f32[128,64]{1,0:T(8,128)S(1)}) custom-call(bf16[2,128,256]{2,1,0:T(8,128)(2,1)S(1)} %bitcast.7, bf16[2,128,256]{2,1,0:T(8,128)(2,1)S(1)} %bitcast.8, bf16[2,128,256]{2,1,0:T(8,128)(2,1)S(1)} %bitcast.9, bf16[128,256]{1,0:T(8,128)(2,1)S(1)} %bitcast.11, bf16[128,256]{1,0:T(8,128)(2,1)S(1)} %copy-done.5, ...), custom_call_target="tpu_custom_call" | custom-call | tf_op jit(solution)/shard_map/pallas_call | solution.py:295
  74.1 0.7 copy.9
  74.8 0.6 copy.11
Async XLA Ops:
  0.6 0.7 copy-start.6
  1.3 0.9 %copy-start = (bf16[1,2,128,256]{3,2,1,0:T(8,128)(2,1)S(1)}, bf16[1,2,128,256]{3,2,1,0:T(8,128)(2,1)}, u32[]{:S(2)}) copy-start(bf16[1,2,128,256]{3,2,1,0:T(8,128)(2,1)} %param.7) | copy-start | bytes 393220
  2.2 0.9 %copy-start.1 = (bf16[1,2,128,256]{3,2,1,0:T(8,128)(2,1)S(1)}, bf16[1,2,128,256]{3,2,1,0:T(8,128)(2,1)}, u32[]{:S(2)}) copy-start(bf16[1,2,128,256]{3,2,1,0:T(8,128)(2,1)} %param.8) | copy-start | bytes 393220
  3.1 0.9 %copy-start.2 = (bf16[1,2,128,256]{3,2,1,0:T(8,128)(2,1)S(1)}, bf16[1,2,128,256]{3,2,1,0:T(8,128)(2,1)}, u32[]{:S(2)}) copy-start(bf16[1,2,128,256]{3,2,1,0:T(8,128)(2,1)} %param.9) | copy-start | bytes 393220
  4.0 0.9 %copy-start.3 = (f32[1,128,256]{2,1,0:T(8,128)S(1)}, f32[1,128,256]{2,1,0:T(8,128)}, u32[]{:S(2)}) copy-start(f32[1,128,256]{2,1,0:T(8,128)} %param.12) | copy-start | bytes 393220
  4.9 0.8 %copy-start.4 = (bf16[1,128,256]{2,1,0:T(8,128)(2,1)S(1)}, bf16[1,128,256]{2,1,0:T(8,128)(2,1)}, u32[]{:S(2)}) copy-start(bf16[1,128,256]{2,1,0:T(8,128)(2,1)} %param.10) | copy-start | bytes 196612
  5.8 0.8 %copy-start.5 = (bf16[128,256]{1,0:T(8,128)(2,1)S(1)}, bf16[128,256]{1,0:T(8,128)(2,1)}, u32[]{:S(2)}) copy-start(bf16[128,256]{1,0:T(8,128)(2,1)} %loss_grad.1) | copy-start | bytes 196612
where the time goes:
time: 75.8 us; the launch traced here: 75.5 us
  Pallas kernels  67.5 us (89%)
  local copies, waits for them, and re-layouts  7.29 us (10%)
    pallas_call x1, Pallas kernels, body(): pl.pallas_call(functools.partial(kernel, sections, n, chans, scale), out_...  67.5 us
    unnamed x16, local copies, waits for them, and re-layouts  7.29 us

commit v1 on v0

v1 whole, which is shorter than its diff:
```python
import functools
import math

import jax
import jax.numpy as jnp
from jax import lax
from jax.experimental import pallas as pl
from jax.experimental.pallas import tpu as pltpu
from jax.sharding import PartitionSpec as P

LANES = 128


def kernel(
    sections,
    n,
    chans,
    scale,
    saved_hbm,
    pre_hbm,
    post_hbm,
    grad_hbm,
    loss_hbm,
    filters_hbm,
    gain_hbm,
    grad_out,
    filter_out,
    saved,
    pre,
    post,
    grad_held,
    loss_grad,
    filters,
    gain,
    send_a,
    recv_a,
    send_b,
    recv_b,
    send_c,
    recv_c,
    send_l,
    send_p,
    recv_p,
    send_d,
    recv_d,
    send_e,
    recv_e,
    send_f,
    recv_f,
    send_g,
    recv_g,
    gain_rows,
    rows,
    padded,
    left,
    hankel,
    result,
    load_sem,
    send_sem,
    recv_sem,
    shift_sem,
):
    section = lax.axis_index("section")
    me = lax.axis_index("seq")
    chan = lax.axis_index("chan")
    width = grad_held.shape[1]
    own = width // n
    per_chan = n // chans
    owner_chan = me // per_chan
    keeps_own = owner_chan == chan
    is_first = section == 0
    is_last = section == sections - 1
    order = sorted(range(1, n), key=lambda off: -min(off, n - off))

    barrier = pltpu.get_barrier_semaphore()
    for off in order:
        pl.semaphore_signal(barrier, inc=1, device_id={"seq": lax.rem(me + off, n)})

    @pl.when(jnp.logical_not(is_last))
    def _():
        pl.semaphore_signal(barrier, inc=1, device_id={"section": section + 1})

    def is_own(slot):
        return (chan * per_chan + slot // chans == me) & (slot % chans == chan)

    def origin(slot):
        return {"seq": chan * per_chan + slot // chans, "chan": jnp.int32(slot % chans)}

    for slot in range(n):

        @pl.when(jnp.logical_not(is_own(slot)))
        def _():
            pl.semaphore_signal(barrier, inc=1, device_id=origin(slot))

    loads = [
        pltpu.make_async_copy(src, dst, load_sem.at[index])
        for index, (src, dst) in enumerate(
            [
                (post_hbm, post),
                (grad_hbm, grad_held),
                (filters_hbm, filters),
                (pre_hbm, pre),
                (saved_hbm, saved),
                (gain_hbm, gain),
                (loss_hbm, loss_grad),
            ]
        )
    ]
    for load in loads:
        load.start()

    row_index = lax.broadcasted_iota(jnp.int32, (LANES, LANES), 0)
    lane_index = lax.broadcasted_iota(jnp.int32, (LANES, LANES), 1)
    flip = (row_index + lane_index == LANES - 1).astype(jnp.bfloat16)
    keep = lane_index <= row_index
    padded[:, n:, :] = jnp.zeros((own, n, LANES), jnp.float32)

    def by_channel(values):
        turned = jnp.transpose(values.astype(jnp.float32)).astype(jnp.bfloat16)
        return turned.reshape(n, own, LANES)

    def flipped(values):
        turned = jnp.transpose(values).astype(jnp.bfloat16)
        turned = jnp.dot(turned, flip, preferred_element_type=jnp.float32)
        return turned.astype(jnp.bfloat16).reshape(n, own, LANES)

    loads[0].wait()
    loads[1].wait()
    gated_0 = post[0].astype(jnp.float32) * grad_held[...].astype(jnp.float32)
    send_a[:, 0] = by_channel(gated_0)
    loads[2].wait()
    send_a[:, 1] = flipped(filters[...])
    loads[3].wait()
    send_b[:, 0] = by_channel(grad_held[...])
    send_b[:, 1] = by_channel(pre[0])
    send_c[...] = by_channel(post[1])
    send_p[...] = by_channel(pre[1])
    loads[4].wait()
    for tick in range(2):
        mixed = pre[tick].astype(jnp.float32) * saved[tick].astype(jnp.float32)
        send_d[:, tick] = flipped(mixed)
    loads[5].wait()
    gain_rows[...] = jnp.transpose(jnp.broadcast_to(gain[...], (LANES, width)))
    loads[6].wait()

    @pl.when(is_last)
    def _():
        send_l[...] = by_channel(loss_grad[...])

    def to_peer(src, dst, phase, off):
        peer = lax.rem(me + off, n)
        return pltpu.make_async_remote_copy(
            src_ref=src.at[peer],
            dst_ref=dst.at[me],
            send_sem=send_sem.at[phase, off],
            recv_sem=recv_sem.at[phase, off],
            device_id={"seq": peer},
        )

    def exchange(src, dst, phase):
        for off in order:
            to_peer(src, dst, phase, off).start()
        dst[me] = src[me]

    def arrive(src, dst, phase):
        for off in order:
            to_peer(src, dst, phase, off).wait_recv()

    def leave(src, dst, phase):
        for off in order:
            to_peer(src, dst, phase, off).wait_send()

    waiting = (
        n
        - 1
        + n
        + jnp.logical_not(is_first).astype(jnp.int32)
        - keeps_own.astype(jnp.int32)
    )
    pl.semaphore_wait(barrier, waiting)

    exchange(send_a, recv_a, 0)
    exchange(send_b, recv_b, 1)
    exchange(send_c, recv_c, 2)

    @pl.when(is_last)
    def _():
        exchange(send_l, recv_g, 3)

    exchange(send_p, recv_p, 4)
    exchange(send_d, recv_d, 5)

    def build_left(block, which):
        for m in range(n):
            padded[:, n - 1 - m, :] = block(m).astype(jnp.float32)

        def one(ch, carry):
            for m in range(n):
                left[which, ch, :, m * LANES : (m + 1) * LANES] = padded[
                    ch, n - 1 - m : 2 * n - 1 - m, :
                ].astype(jnp.bfloat16)
            return carry

        lax.fori_loop(0, own, one, 0)

    def correlate(tick):
        def one(ch, carry):
            held = rows[ch]

            def turned(m):
                spread = jnp.broadcast_to(held[m : m + 1], (LANES, LANES))
                return pltpu.roll(spread, 1, 1, stride=1, stride_axis=0)

            now = turned(0)
            for m in range(n):
                later = turned(m + 1) if m + 1 < n else jnp.zeros_like(now)
                hankel[tick, ch, m * LANES : (m + 1) * LANES, :] = jnp.where(
                    keep, now, later
                ).astype(jnp.bfloat16)
                now = later
            result[ch] = jnp.dot(
                left[0, ch], hankel[tick, ch], preferred_element_type=jnp.float32
            )
            return carry

        lax.fori_loop(0, own, one, 0)

    def lag_products():
        def one(ch, carry):
            result[ch] = jnp.dot(
                left[1, ch], hankel[0, ch], preferred_element_type=jnp.float32
            ) + jnp.dot(left[2, ch], hankel[1, ch], preferred_element_type=jnp.float32)
            return carry

        lax.fori_loop(0, own, one, 0)

    my_gain = gain_rows[pl.ds(pl.multiple_of(me * own, own), own), :]

    def combined(held, gate, gated, m):
        inner = result[:, m, :] + my_gain * gated
        total = held.astype(jnp.float32) + gate.astype(jnp.float32) * inner
        return total.astype(jnp.bfloat16)

    arrive(send_a, recv_a, 0)
    for m in range(n):
        rows[:, m, :] = recv_a[m, 0].astype(jnp.float32)
    build_left(lambda m: recv_a[m, 1], 0)
    correlate(0)
    arrive(send_b, recv_b, 1)
    for m in range(n):
        send_g[m] = combined(recv_b[m, 0], recv_b[m, 1], recv_a[m, 0].astype(jnp.float32), m)
    shift = pltpu.make_async_remote_copy(
        src_ref=send_g,
        dst_ref=recv_g,
        send_sem=shift_sem.at[0],
        recv_sem=shift_sem.at[1],
        device_id={"section": lax.rem(section + sections - 1, sections)},
    )

    @pl.when(jnp.logical_not(is_first))
    def _():
        shift.start()

    arrive(send_c, recv_c, 2)

    @pl.when(jnp.logical_not(is_last))
    def _():
        shift.wait_recv()

    @pl.when(is_last)
    def _():
        arrive(send_l, recv_g, 3)

    for m in range(n):
        rows[:, m, :] = recv_c[m].astype(jnp.float32) * recv_g[m].astype(jnp.float32)
    correlate(1)
    arrive(send_p, recv_p, 4)
    for m in range(n):
        send_e[m] = combined(recv_g[m], recv_p[m], rows[:, m, :], m)
    exchange(send_e, recv_e, 6)
    arrive(send_d, recv_d, 5)
    build_left(lambda m: recv_d[m, 0], 1)
    build_left(lambda m: recv_d[m, 1], 2)
    lag_products()
    for m in range(n):
        send_f[m] = result[:, m, :].astype(jnp.bfloat16)

    landing = lax.rem(me, per_chan) * chans + chan

    def deliver(off):
        target = lax.rem(me + off, n)
        return pltpu.make_async_remote_copy(
            src_ref=send_f.at[target],
            dst_ref=recv_f.at[landing],
            send_sem=send_sem.at[7, off],
            recv_sem=recv_sem.at[7, landing],
            device_id={"seq": target, "chan": owner_chan},
        )

    for off in order:
        deliver(off).start()

    @pl.when(jnp.logical_not(keeps_own))
    def _():
        deliver(0).start()

    @pl.when(keeps_own)
    def _():
        recv_f[landing] = send_f[me]

    arrive(send_e, recv_e, 6)
    gradient = recv_e[...].astype(jnp.float32).reshape(width, LANES)
    grad_out[...] = jnp.transpose(gradient).astype(jnp.bfloat16)

    leave(send_a, recv_a, 0)
    leave(send_b, recv_b, 1)
    leave(send_c, recv_c, 2)

    @pl.when(is_last)
    def _():
        leave(send_l, recv_g, 3)

    leave(send_p, recv_p, 4)
    leave(send_d, recv_d, 5)
    leave(send_e, recv_e, 6)

    @pl.when(jnp.logical_not(is_first))
    def _():
        shift.wait_send()

    for slot in range(n):

        @pl.when(jnp.logical_not(is_own(slot)))
        def _():
            pltpu.make_async_remote_copy(
                src_ref=send_f.at[0],
                dst_ref=recv_f.at[slot],
                send_sem=send_sem.at[7, 0],
                recv_sem=recv_sem.at[7, slot],
                device_id=origin(slot),
            ).wait_recv()

    pieces = recv_f[...].astype(jnp.float32).reshape(per_chan, chans, own, LANES)
    filter_out[...] = jnp.sum(pieces, axis=1).reshape(per_chan * own, LANES) * scale

    for off in order:
        deliver(off).wait_send()

    @pl.when(jnp.logical_not(keeps_own))
    def _():
        deliver(0).wait_send()


def body(mesh, saved_input, pre_gate, post_gate, grad_held, loss_grad, filters, skip_gain):
    sections, n, chans = (mesh.shape[axis] for axis in ("section", "seq", "chan"))
    ticks, rows, width = saved_input.shape[1:]
    own = width // n
    length = rows * n
    scale = 1.0 / math.sqrt(length * chans * ticks)
    pair = pltpu.VMEM((n, 2, own, rows), jnp.bfloat16)
    single = pltpu.VMEM((n, own, rows), jnp.bfloat16)
    both = pltpu.VMEM((ticks, rows, width), jnp.bfloat16)
    block = pltpu.VMEM((rows, width), jnp.bfloat16)
    vmem = pl.BlockSpec(memory_space=pltpu.VMEM)
    hbm = pl.BlockSpec(memory_space=pltpu.HBM)
    gradient, lag_grad = pl.pallas_call(
        functools.partial(kernel, sections, n, chans, scale),
        out_shape=(
            jax.ShapeDtypeStruct((rows, width), jnp.bfloat16),
            jax.ShapeDtypeStruct((width // chans, rows), jnp.float32),
        ),
        in_specs=[hbm] * 7,
        out_specs=(vmem, vmem),
        scratch_shapes=[both] * 3
        + [block] * 2
        + [
            pltpu.VMEM((rows, width), jnp.float32),
            pltpu.VMEM((1, width), jnp.float32),
        ]
        + [pair] * 4
        + [single] * 5
        + [pair] * 2
        + [single] * 6
        + [
            pltpu.VMEM((width, rows), jnp.float32),
            pltpu.VMEM((own, n, rows), jnp.float32),
            pltpu.VMEM((own, 2 * n, rows), jnp.float32),
            pltpu.VMEM((3, own, n, length), jnp.bfloat16),
            pltpu.VMEM((ticks, own, length, rows), jnp.bfloat16),
            pltpu.VMEM((own, n, rows), jnp.float32),
            pltpu.SemaphoreType.DMA((7,)),
            pltpu.SemaphoreType.DMA((8, n)),
            pltpu.SemaphoreType.DMA((8, n)),
            pltpu.SemaphoreType.DMA((2,)),
        ],
        compiler_params=pltpu.CompilerParams(
            collective_id=0, has_side_effects=True, vmem_limit_bytes=67_043_328
        ),
    )(
        saved_input[0],
        pre_gate[0],
        post_gate[0],
        grad_held[0],
        loss_grad,
        filters[0],
        skip_gain,
    )
    return gradient[None], jnp.transpose(lag_grad)[None]


def solution(mesh):
    placed = (
        P("section", None, "seq", "chan"),
        P("section", None, "seq", "chan"),
        P("section", None, "seq", "chan"),
        P("section", "seq", "chan"),
        P("seq", "chan"),
        P("section", "seq", None),
        P("section", None),
    )
    return jax.shard_map(
        functools.partial(body, mesh),
        mesh=mesh,
        in_specs=placed,
        out_specs=(P("section", "seq", "chan"), P("section", "seq", "chan")),
        check_vma=False,
    )
```

time: 75.8 us -> 60.3 us (0.80)
  Pallas kernels: 67.5 us -> 57.4 us
  local copies, waits for them, and re-layouts: 7.29 us -> 2.1 us
    pallas_call x1, Pallas kernels: 67.5 us -> 57.4 us  [body(): pl.pallas_call(functools.partial(kernel, sections, n, chans, scale), out_...]
    unnamed x16 -> x4, local copies, waits for them, and re-layouts: 7.29 us -> 2.1 us
where the time goes in v1:
time: 60.3 us; the launch traced here: 60.2 us
  Pallas kernels  57.4 us (95%)
  local copies, waits for them, and re-layouts  2.1 us (3%)
  between operations  0.65 us (1%)
    pallas_call x1, Pallas kernels, body(): pl.pallas_call(functools.partial(kernel, sections, n, chans, scale), out_...  57.4 us
    unnamed x4, local copies, waits for them, and re-layouts  2.1 us

profile of v1, /device:TPU:19, one launch (start us, length us, event | category | flops | bytes accessed | tf_op | source)
XLA Modules:
  0.0 60.2 jit_solution(2532705365743457487)
XLA Ops:
  0.6 57.4 %shard_map.86 = (bf16[128,256]{1,0:T(8,128)(2,1)}, f32[64,128]{1,0:T(8,128)}) custom-call(bf16[2,128,256]{2,1,0:T(8,128)(2,1)} %bitcast.9, bf16[2,128,256]{2,1,0:T(8,128)(2,1)} %bitcast.10, bf16[2,128,256]{2,1,0:T(8,128)(2,1)} %bitcast.11, bf16[128,256]{1,0:T(8,128)(2,1)} %bitcast.13, bf16[128,256]{1,0:T(8,128)(2,1)} %loss_hbm.1, f32[128,256]{1,0:T(8,128)} %bitcast.12, ...), custom_call_target="tpu_custom_call" | custom-call | tf_op jit(solution)/shard_map/pallas_call | solution.py:366
  58.0 0.0 copy-start
  58.1 1.5 %copy.11 = bf16[1,128,256]{2,1,0:T(8,128)(2,1)} copy(bf16[1,128,256]{2,1,0:T(8,128)(2,1)} %bitcast.14) | data formatting | bytes 131072
  59.5 0.0 copy-done
  59.5 0.6 %copy.12 = f32[1,128,64]{1,2,0:T(8,128)} copy(f32[1,128,64]{1,2,0:T(8,128)S(1)} %bitcast.15) | data formatting | bytes 65536
Async XLA Ops:
  58.0 1.5 %copy-start = (f32[64,128]{1,0:T(8,128)S(1)}, f32[64,128]{1,0:T(8,128)}, u32[]{:S(2)}) copy-start(f32[64,128]{1,0:T(8,128)} %get-tuple-element.5) | copy-start | bytes 98308

commit v2 on v1

--- a/solution.py
+++ b/solution.py
@@ -38,7 +38,6 @@
     recv_b,
     send_c,
     recv_c,
-    send_l,
     send_p,
     recv_p,
     send_d,
@@ -133,7 +132,6 @@
     loads[3].wait()
     send_b[:, 0] = by_channel(grad_held[...])
     send_b[:, 1] = by_channel(pre[0])
-    send_c[...] = by_channel(post[1])
     send_p[...] = by_channel(pre[1])
     loads[4].wait()
     for tick in range(2):
@@ -145,7 +143,12 @@
 
     @pl.when(is_last)
     def _():
-        send_l[...] = by_channel(loss_grad[...])
+        held = loss_grad[...].astype(jnp.float32)
+        send_c[...] = by_channel(post[1].astype(jnp.float32) * held)
+
+    @pl.when(jnp.logical_not(is_last))
+    def _():
+        send_c[...] = by_channel(post[1])
 
     def to_peer(src, dst, phase, off):
         peer = lax.rem(me + off, n)
@@ -183,11 +186,11 @@
     exchange(send_b, recv_b, 1)
     exchange(send_c, recv_c, 2)
 
-    @pl.when(is_last)
-    def _():
-        exchange(send_l, recv_g, 3)
-
-    exchange(send_p, recv_p, 4)
+
+    @pl.when(jnp.logical_not(is_last))
+    def _():
+        exchange(send_p, recv_p, 4)
+
     exchange(send_d, recv_d, 5)
 
     def build_left(block, which):
@@ -201,7 +204,7 @@
                 ].astype(jnp.bfloat16)
             return carry
 
-        lax.fori_loop(0, own, one, 0)
+        lax.fori_loop(0, own, one, 0, unroll=4)
 
     def correlate(tick):
         def one(ch, carry):
@@ -223,7 +226,7 @@
             )
             return carry
 
-        lax.fori_loop(0, own, one, 0)
+        lax.fori_loop(0, own, one, 0, unroll=4)
 
     def lag_products():
         def one(ch, carry):
@@ -232,7 +235,7 @@
             ) + jnp.dot(left[2, ch], hankel[1, ch], preferred_element_type=jnp.float32)
             return carry
 
-        lax.fori_loop(0, own, one, 0)
+        lax.fori_loop(0, own, one, 0, unroll=4)
 
     my_gain = gain_rows[pl.ds(pl.multiple_of(me * own, own), own), :]
 
@@ -266,17 +269,26 @@
     @pl.when(jnp.logical_not(is_last))
     def _():
         shift.wait_recv()
+        for m in range(n):
+            rows[:, m, :] = recv_c[m].astype(jnp.float32) * recv_g[m].astype(jnp.float32)
 
     @pl.when(is_last)
     def _():
-        arrive(send_l, recv_g, 3)
-
-    for m in range(n):
-        rows[:, m, :] = recv_c[m].astype(jnp.float32) * recv_g[m].astype(jnp.float32)
+        for m in range(n):
+            rows[:, m, :] = recv_c[m].astype(jnp.float32)
+
     correlate(1)
-    arrive(send_p, recv_p, 4)
-    for m in range(n):
-        send_e[m] = combined(recv_g[m], recv_p[m], rows[:, m, :], m)
+    @pl.when(jnp.logical_not(is_last))
+    def _():
+        arrive(send_p, recv_p, 4)
+        for m in range(n):
+            send_e[m] = combined(recv_g[m], recv_p[m], rows[:, m, :], m)
+
+    @pl.when(is_last)
+    def _():
+        for m in range(n):
+            send_e[m] = result[:, m, :].astype(jnp.bfloat16)
+
     exchange(send_e, recv_e, 6)
     arrive(send_d, recv_d, 5)
     build_left(lambda m: recv_d[m, 0], 1)
@@ -309,18 +321,27 @@
         recv_f[landing] = send_f[me]
 
     arrive(send_e, recv_e, 6)
-    gradient = recv_e[...].astype(jnp.float32).reshape(width, LANES)
-    grad_out[...] = jnp.transpose(gradient).astype(jnp.bfloat16)
+    back = jnp.transpose(recv_e[...].astype(jnp.float32).reshape(width, LANES))
+
+    @pl.when(jnp.logical_not(is_last))
+    def _():
+        grad_out[...] = back.astype(jnp.bfloat16)
+
+    @pl.when(is_last)
+    def _():
+        held = loss_grad[...].astype(jnp.float32)
+        gated = post[1].astype(jnp.float32) * held
+        inner = back + gain[...] * gated
+        grad_out[...] = (held + pre[1].astype(jnp.float32) * inner).astype(jnp.bfloat16)
 
     leave(send_a, recv_a, 0)
     leave(send_b, recv_b, 1)
     leave(send_c, recv_c, 2)
 
-    @pl.when(is_last)
-    def _():
-        leave(send_l, recv_g, 3)
-
-    leave(send_p, recv_p, 4)
+    @pl.when(jnp.logical_not(is_last))
+    def _():
+        leave(send_p, recv_p, 4)
+
     leave(send_d, recv_d, 5)
     leave(send_e, recv_e, 6)
 
@@ -378,7 +399,7 @@
             pltpu.VMEM((1, width), jnp.float32),
         ]
         + [pair] * 4
-        + [single] * 5
+        + [single] * 4
         + [pair] * 2
         + [single] * 6
         + [

time: 60.3 us -> 57.3 us (0.950)
  the two profiles are of different devices: /device:TPU:19 before, /device:TPU:20 now
where the time goes in v2:
time: 57.3 us; the launch traced here: 57.1 us
  Pallas kernels  54.4 us (95%)
  local copies, waits for them, and re-layouts  2.1 us (4%)
  between operations  0.65 us (1%)
    pallas_call x1, Pallas kernels, body(): pl.pallas_call(functools.partial(kernel, sections, n, chans, scale), out_...  54.4 us
    unnamed x4, local copies, waits for them, and re-layouts  2.1 us

profile of v2, /device:TPU:20, one launch (start us, length us, event | category | flops | bytes accessed | tf_op | source)
XLA Modules:
  0.0 57.1 jit_solution(8904066509703885995)
XLA Ops:
  0.6 54.4 %shard_map.86 = (bf16[128,256]{1,0:T(8,128)(2,1)}, f32[64,128]{1,0:T(8,128)}) custom-call(bf16[2,128,256]{2,1,0:T(8,128)(2,1)} %bitcast.9, bf16[2,128,256]{2,1,0:T(8,128)(2,1)} %bitcast.10, bf16[2,128,256]{2,1,0:T(8,128)(2,1)} %bitcast.11, bf16[128,256]{1,0:T(8,128)(2,1)} %bitcast.13, bf16[128,256]{1,0:T(8,128)(2,1)} %loss_hbm.1, f32[128,256]{1,0:T(8,128)} %bitcast.12, ...), custom_call_target="tpu_custom_call" | custom-call | tf_op jit(solution)/shard_map/pallas_call | solution.py:387
  55.0 0.0 copy-start
  55.0 1.5 %copy.11 = bf16[1,128,256]{2,1,0:T(8,128)(2,1)} copy(bf16[1,128,256]{2,1,0:T(8,128)(2,1)} %bitcast.14) | data formatting | bytes 131072
  56.5 0.0 copy-done
  56.5 0.6 %copy.12 = f32[1,128,64]{1,2,0:T(8,128)} copy(f32[1,128,64]{1,2,0:T(8,128)S(1)} %bitcast.15) | data formatting | bytes 65536
Async XLA Ops:
  55.0 1.5 %copy-start = (f32[64,128]{1,0:T(8,128)S(1)}, f32[64,128]{1,0:T(8,128)}, u32[]{:S(2)}) copy-start(f32[64,128]{1,0:T(8,128)} %get-tuple-element.5) | copy-start | bytes 98308
